TPU v7x, 32 devices: a whole 2x2x4 slice. The times are simulated.
32 devices in a mesh: ctx: 4 (over z), tp: 2 (over x), dp: 4 (over y, core).
Axes of the slice: x: 2, y: 2, z: 4, core: 2. Of those that a mesh axis runs over, the one named last changes fastest.
Arguments:
- queries: bfloat16 [4, 1024, 8192], P('dp', 'ctx', 'tp'), may hold values from -80 to 80
- prompt_keys: bfloat16 [4, 1024, 1024], P('dp', 'ctx', 'tp'), may hold values from -4 to 4
- prompt_values: bfloat16 [4, 1024, 1024], P('dp', 'ctx', 'tp'), may hold values from -6 to 6
- resp_keys: bfloat16 [4, 1024, 1024], P('dp', 'ctx', 'tp'), may hold values from -4 to 4
- resp_values: bfloat16 [4, 1024, 1024], P('dp', 'ctx', 'tp'), may hold values from -6 to 6
- pattern: int32 [4, 2, 8], P('dp'), may hold values from 0 to 1, as said below
- lengths: int32 [4, 2], P('dp'), may hold values from 257 to 512, as said below
- out_weight: bfloat16 [8192, 4096], P(('tp', 'dp'), 'ctx'), may hold values from -0.0625 to 0.0625
Outputs:
- attended: bfloat16 [4, 1024, 4096], P('dp', 'ctx', 'tp')
Inputs may be any that keep to these rules, and one draw needn't show every extreme that they name: pattern[g, r, 0] is 1 for every response; each response reads 4 or more blocks; in each group some response reads all 8 blocks. `lengths`: in each group some response has length 512.
All inputs are finite; a program needn't handle non-finite values.
Results may differ from a plain program's by a relative error of at most 0.013.
Values may be sent and summed in bfloat16 or wider, within the bound.
A program may use at most 192 MiB of HBM per device.

v0:
```python
import jax
import jax.numpy as jnp
from jax import lax
from jax.sharding import PartitionSpec as P

HD = 128
BLK = 128
RLEN = 512


def shifted(x, axis, by):
    devices = lax.axis_size(axis)
    pairs = [(i, i + by) for i in range(devices) if 0 <= i + by < devices]
    return lax.ppermute(x, axis, pairs)


def local(
    queries, prompt_keys, prompt_values, resp_keys, resp_values, pattern, lengths, out_weight
):
    tok = queries.shape[1]
    kv_here = prompt_keys.shape[2] // HD
    q_here = queries.shape[2] // HD
    group = q_here // kv_here
    scale = HD ** (-0.5)
    halves = RLEN // tok
    responses = lax.axis_size("ctx") // halves
    place = lax.axis_index("ctx")
    resp_id = place % responses
    half = place // responses
    positions = half * tok + jnp.arange(tok, dtype=jnp.int32)
    chosen = jnp.arange(pattern.shape[1], dtype=jnp.int32) == resp_id
    block_row = jnp.sum(jnp.where(chosen[:, None], pattern[0], 0), axis=0)
    live_len = jnp.sum(jnp.where(chosen, lengths[0], 0))
    query_heads = queries[0].reshape(tok, kv_here, group, HD)
    earlier = shifted((resp_keys, resp_values), "ctx", responses)
    own_keys = jnp.concatenate([earlier[0][0], resp_keys[0]], axis=0).reshape(2 * tok, kv_here, HD)
    own_vals = jnp.concatenate([earlier[1][0], resp_values[0]], axis=0).reshape(
        2 * tok, kv_here, HD
    )
    key_pos = (half - 1) * tok + jnp.arange(2 * tok, dtype=jnp.int32)
    allowed = (key_pos[None, :] >= 0) & (key_pos[None, :] <= positions[:, None])
    scores = (
        jnp.einsum("ikgd,jkd->kgij", query_heads, own_keys, preferred_element_type=jnp.float32)
        * scale
    )
    running = jnp.max(jnp.where(allowed, scores, -jnp.inf), axis=-1)
    probs = jnp.where(allowed, jnp.exp(scores - running[..., None]), 0.0)
    total = jnp.sum(probs, axis=-1)
    accum = jnp.einsum(
        "kgij,jkd->kgid", probs.astype(jnp.bfloat16), own_vals, preferred_element_type=jnp.float32
    )
    pieces = (
        lax.all_gather(prompt_keys, "ctx", axis=1, tiled=True),
        lax.all_gather(prompt_values, "ctx", axis=1, tiled=True),
    )
    count = pieces[0].shape[1]
    block_ids = jnp.arange(count, dtype=jnp.int32) // BLK
    onehot = block_ids[:, None] == jnp.arange(block_row.shape[0], dtype=jnp.int32)[None, :]
    readable = jnp.sum(jnp.where(onehot, block_row[None, :], 0), axis=1) > 0
    piece_keys = pieces[0][0].reshape(-1, kv_here, HD)
    piece_vals = pieces[1][0].reshape(-1, kv_here, HD)
    block_scores = (
        jnp.einsum("ikgd,jkd->kgij", query_heads, piece_keys, preferred_element_type=jnp.float32)
        * scale
    )
    mask = readable[None, None, None, :]
    new_max = jnp.maximum(running, jnp.max(jnp.where(mask, block_scores, -jnp.inf), axis=-1))
    weights = jnp.where(mask, jnp.exp(block_scores - new_max[..., None]), 0.0)
    factor = jnp.exp(running - new_max)
    new_total = total * factor + jnp.sum(weights, axis=-1)
    new_acc = accum * factor[..., None] + jnp.einsum(
        "kgij,jkd->kgid",
        weights.astype(jnp.bfloat16),
        piece_vals,
        preferred_element_type=jnp.float32,
    )
    context = new_acc / new_total[..., None]
    context = jnp.transpose(context, (2, 0, 1, 3)).reshape(tok, q_here * HD)
    context = jnp.where((positions < live_len)[:, None], context, 0.0).astype(jnp.bfloat16)
    head_rows = lax.all_gather(out_weight, "dp", axis=0, tiled=True)
    rows = lax.all_gather(context, "ctx", axis=0, tiled=True)
    columns = jnp.dot(rows, head_rows, preferred_element_type=jnp.float32).astype(jnp.bfloat16)
    partial_out = lax.all_to_all(columns, "ctx", split_axis=0, concat_axis=1, tiled=True)
    summed = lax.psum_scatter(partial_out, "tp", scatter_dimension=1, tiled=True)
    return summed[None]


def solution(mesh):
    placed = (
        P("dp", "ctx", "tp"),
        P("dp", "ctx", "tp"),
        P("dp", "ctx", "tp"),
        P("dp", "ctx", "tp"),
        P("dp", "ctx", "tp"),
        P("dp", None, None),
        P("dp", None),
        P(("tp", "dp"), "ctx"),
    )
    return jax.shard_map(
        local, mesh=mesh, in_specs=placed, out_specs=P("dp", "ctx", "tp"), check_vma=False
    )
```

profile of v0, /device:TPU:0, one launch (start us, length us, event | category | flops | bytes accessed | tf_op | source)
XLA Modules:
  0.0 398.9 jit_solution(16821264540768724130)
XLA Ops:
  6.5 0.0 all-gather.5.cloned.1.call-start
  6.5 1.8 copy.39
  8.3 0.0 all-gather.5.cloned.1.call-update
  8.4 0.0 all-gather.7.cloned.1.call-start
  8.4 0.7 all-gather.7.cloned.1.call-update
  9.1 0.0 all-gather.11.cloned.1.call-start
  9.2 0.7 all-gather.11.cloned.1.call-update
  9.8 0.0 all-gather.9.cloned.1.call-start
  9.9 1.1 copy.31
  11.0 6.0 %collective-permute-start = (bf16[1,256,512]{1,2,0:T(8,128)(2,1)S(1)}, bf16[1,256,512]{1,2,0:T(8,128)(2,1)S(1)}, u32[]{:S(2)}, u32[]{:S(2)}) collective-permute-start(bf16[1,256,512]{1,2,0:T(8,128)(2,1)S(1)} %copy.31), channel_id=1, source_target_pairs={{0,16},{8,24},{1,17},{9,25},{2,18},{10,26},{3,19},{11,27},{4,20},{... | collective-permute-start | bytes 786440 | tf_op jit(solution)/shard_map/ppermute | solution.py:14
  17.0 1.3 collective-permute-start.1
  18.3 0.6 broadcast_compare_fusion.1
  18.9 1.3 fusion.33
  20.2 0.8 fusion.32
  21.0 0.1 select_reduce_fusion
  21.1 0.6 broadcast_compare_fusion.2
  21.7 1.1 copy.37
  22.7 2.1 copy.54
  24.8 0.2 copy.34
  25.0 0.9 compare_and_fusion
  25.9 1.8 collective-permute-done
  27.7 0.2 copy.33
  27.8 10.0 %collective-permute-done.1 = bf16[1,256,512]{2,1,0:T(8,128)(2,1)S(1)} collective-permute-done((bf16[1,256,512]{2,1,0:T(8,128)(2,1)}, bf16[1,256,512]{2,1,0:T(8,128)(2,1)S(1)}, u32[]{:S(2)}, u32[]{:S(2)}) %collective-permute-start.1) | collective-permute-done | bytes 262176 | tf_op jit(solution)/shard_map/ppermute | solution.py:14
  37.9 0.1 copy.36
  38.0 7.2 %fusion.5 = (f32[4,8,256]{2,1,0:T(8,128)S(1)}, f32[4,512,256,8]{2,1,3,0:T(8,128)}) fusion(pred[256,512]{0,1:T(8,128)(4,1)S(1)} %compare_and_fusion, bf16[256,4,8,128]{3,2,1,0:T(8,128)(2,1)S(1)} %bitcast.101, bf16[256,4,128]{2,0,1:T(8,128)(2,1)S(1)} %copy.34, bf16[256,4,128]{2,0,1:T(8,128)(2,1)S(1)} %copy.33), kind=kOutput, calls=%fused_computation.9 | convolution fusion | flops 1087365120 | bytes 19562496 | tf_op jit(solution)/shard_map/ikgd,jkd->kgij/dot_general | solution.py:43
  45.2 9.2 %fusion.11 = f32[4,8,256]{2,1,0:T(8,128)S(1)} fusion(f32[4,512,256,8]{2,1,3,0:T(8,128)} %get-tuple-element.8, f32[4,8,256]{2,1,0:T(8,128)S(1)} %get-tuple-element.7, pred[256,512]{0,1:T(8,128)(4,1)S(1)} %compare_and_fusion), kind=kLoop, calls=%fused_computation.14 | loop fusion | flops 16769024 | bytes 16973824 | tf_op jit(solution)/shard_map/reduce_sum | solution.py:48
  54.3 0.0 all-gather.5.cloned.1.call-done
  54.4 16.1 %fusion = (f32[4,8,256]{2,1,0:T(8,128)S(1)}, f32[4,1024,256,8]{2,1,3,0:T(8,128)}) fusion(pred[1024]{0:T(1024)(128)(4,1)S(1)} %broadcast_compare_fusion, bf16[1024,4,128,1]{0,2,3,1:T(8,128)(2,1)} %bitcast.107, bf16[256,4,8,128]{3,2,1,0:T(8,128)(2,1)S(1)} %bitcast.102), kind=kOutput, calls=%fused_computation.2 | convolution fusion | flops 2172641280 | bytes 36733952 | tf_op jit(solution)/shard_map/ikgd,jkd->kgij/dot_general | solution.py:63
  70.4 14.8 %all-gather.7.cloned.1.call-done = bf16[1,1024,512]{2,1,0:T(8,128)(2,1)} async-done(((bf16[1,256,512]{2,1,0:T(8,128)(2,1)}), bf16[1,1024,512]{2,1,0:T(8,128)(2,1)}) %all-gather.7.cloned.1.call-update) | async-done | bytes 1048592 | tf_op jit(solution)/shard_map/all_gather | solution.py:54
  85.2 1.5 copy.42
  86.7 15.7 %fusion.3 = f32[4,8,256]{2,1,0:T(8,128)S(1)} fusion(f32[4,1024,256,8]{2,1,3,0:T(8,128)} %get-tuple-element.10, f32[4,8,256]{2,1,0:T(8,128)S(1)} %max.18, pred[1024]{0:T(1024)(128)(4,1)S(1)} %broadcast_compare_fusion), kind=kLoop, calls=%fused_computation.5 | loop fusion | flops 33546240 | bytes 33620992 | tf_op jit(solution)/shard_map/reduce_sum | solution.py:70
  102.4 14.2 %fusion.8 = f32[4,8,256,128]{2,3,1,0:T(8,128)S(1)} fusion(bf16[1024,4,128,1]{0,2,3,1:T(8,128)(2,1)S(1)} %bitcast.108, f32[4,1024,256,8]{2,1,3,0:T(8,128)} %get-tuple-element.10, f32[4,8,256]{2,1,0:T(8,128)S(1)} %max.18, pred[1024]{0:T(1024)(128)(4,1)S(1)} %broadcast_compare_fusion), kind=kOutput, calls=%fused_computation.12 | convolution fusion | flops 2181038080 | bytes 38831104 | tf_op jit(solution)/shard_map/kgij,jkd->kgid/dot_general | solution.py:71
  116.6 7.9 %fusion.17 = bf16[256,4,8,128]{0,3,2,1:T(8,128)(2,1)S(1)} fusion(f32[4,8,256,128]{2,3,1,0:T(8,128)S(1)} %fusion.8, f32[4,512,256,8]{2,1,3,0:T(8,128)} %get-tuple-element.8, f32[4,8,256]{2,1,0:T(8,128)S(1)} %get-tuple-element.7, pred[256,512]{0,1:T(8,128)(4,1)S(1)} %compare_and_fusion, f32[256,4,8]{0,2,1:T(8,128)S(1)} %get-tuple-element.5, ...), kind=kOutput, calls=%fused_computation.21 | convolution fusion | flops 1095761920 | bytes 23822336 | tf_op jit(solution)/shard_map/kgij,jkd->kgid/dot_general | solution.py:49
  124.6 1.9 fusion.16
  126.5 0.0 all-gather.9.cloned.1.call-update
  126.5 0.0 reduce-scatter.2.cloned.1.call-start
  126.6 17.9 %all-gather.11.cloned.1.call-done = bf16[4096,1024]{1,0:T(8,128)(2,1)} async-done(((bf16[1024,1024]{1,0:T(8,128)(2,1)}), bf16[4096,1024]{1,0:T(8,128)(2,1)}) %all-gather.11.cloned.1.call-update) | async-done | bytes 8388624 | tf_op jit(solution)/shard_map/all_gather | solution.py:80
  144.5 150.6 %all-gather.9.cloned.1.call-done = bf16[1024,4096]{0,1:T(8,128)(2,1)} async-done(((bf16[256,4096]{0,1:T(8,128)(2,1)}), bf16[1024,4096]{0,1:T(8,128)(2,1)}) %all-gather.9.cloned.1.call-update) | async-done | bytes 8388624 | tf_op jit(solution)/shard_map/all_gather | solution.py:81
  295.0 13.7 %convolution_convert_fusion = bf16[1024,1024]{1,0:T(8,128)(2,1)S(1)} fusion(bf16[1024,4096]{0,1:T(8,128)(2,1)} %all-gather.9.cloned.1.call-done, bf16[4096,1024]{1,0:T(8,128)(2,1)} %all-gather.11.cloned.1.call-done), kind=kOutput, calls=%fused_computation.23 | convolution fusion | flops 8590983168 | bytes 18874368 | tf_op jit(solution)/shard_map/dot_general | solution.py:82
  308.8 50.8 %all_to_all.19 = bf16[4,256,1024]{2,1,0:T(8,128)(2,1)S(1)} all-to-all(bf16[4,256,1024]{2,1,0:T(8,128)(2,1)S(1)} %bitcast.106), channel_id=1, replica_groups=mesh['ctx'=4,'tp'=2,'dp'=4] {'ctx'}, dimensions={0} | all-to-all | bytes 4194304 | tf_op jit(solution)/shard_map/all_to_all | solution.py:83
  359.5 1.5 copy.53
  361.1 0.0 reduce-scatter.2.cloned.1.call-update
  361.1 31.3 %reduce-scatter.2.cloned.1.call-done = bf16[256,2048]{1,0:T(8,128)(2,1)} async-done(((bf16[256,4096]{1,0:T(8,128)(2,1)}), bf16[256,2048]{1,0:T(8,128)(2,1)}) %reduce-scatter.2.cloned.1.call-update) | async-done | bytes 1048592 | tf_op jit(solution)/shard_map/reduce_scatter | solution.py:84
  (7 shorter events, 0.0 us)
Async XLA Ops:
  6.5 47.8 %all-gather.5.cloned.1.call-start = ((), (), s32[]{:S(2)}) async-start(), calls=%async_computation.2 | async-start | bytes 1310720 | tf_op jit(solution)/shard_map/all_gather | solution.py:53
  8.4 76.9 %all-gather.7.cloned.1.call-start = ((), (), s32[]{:S(2)}) async-start(), calls=%async_computation.3 | async-start | bytes 1310720 | tf_op jit(solution)/shard_map/all_gather | solution.py:54
  9.1 135.4 %all-gather.11.cloned.1.call-start = ((), (), s32[]{:S(2)}) async-start(), calls=%async_computation.5 | async-start | bytes 10485760 | tf_op jit(solution)/shard_map/all_gather | solution.py:80
  9.8 285.2 %all-gather.9.cloned.1.call-start = ((), (), s32[]{:S(2)}) async-start(), calls=%async_computation.4 | async-start | bytes 10485760 | tf_op jit(solution)/shard_map/all_gather | solution.py:81
  11.0 16.7 %collective-permute-start = (bf16[1,256,512]{1,2,0:T(8,128)(2,1)S(1)}, bf16[1,256,512]{1,2,0:T(8,128)(2,1)S(1)}, u32[]{:S(2)}, u32[]{:S(2)}) collective-permute-start(bf16[1,256,512]{1,2,0:T(8,128)(2,1)S(1)} %copy.31), channel_id=1, source_target_pairs={{0,16},{8,24},{1,17},{9,25},{2,18},{10,26},{3,19},{11,27},{4,20},{... | collective-permute-start | bytes 786440 | tf_op jit(solution)/shard_map/ppermute | solution.py:14
  17.0 20.9 %collective-permute-start.1 = (bf16[1,256,512]{2,1,0:T(8,128)(2,1)}, bf16[1,256,512]{2,1,0:T(8,128)(2,1)S(1)}, u32[]{:S(2)}, u32[]{:S(2)}) collective-permute-start(bf16[1,256,512]{2,1,0:T(8,128)(2,1)} %param.12), channel_id=1, source_target_pairs={{0,16},{8,24},{1,17},{9,25},{2,18},{10,26},{3,19},{11,27},{4,20},{... | collective-permute-start | bytes 786440 | tf_op jit(solution)/shard_map/ppermute | solution.py:14
  126.5 265.9 %reduce-scatter.2.cloned.1.call-start = ((), (), s32[]{:S(2)}) async-start(), calls=%async_computation.6 | async-start | bytes 3145728 | tf_op jit(solution)/shard_map/reduce_scatter | solution.py:84
Sparse Core Ops, SparseCore 0:
  8.9 44.7 all-gather.4
  55.2 29.9 all-gather.6
  86.8 57.6 all-gather.10
  145.9 149.0 all-gather.8
  361.2 31.1 reduce-scatter.1
where the time goes:
time: 399 us
  waiting for transfers between devices  228 us (57%)
  matrix products  59.1 us (15%)
  blocking collectives  50.8 us (13%)
  other arithmetic  31 us (8%)
  between operations  13.3 us (3%)
  local copies, waits for them, and re-layouts  9.5 us (2%)
  starting transfers between devices  7.45 us (2%)
    all_gather x1, waiting for transfers between devices, local(): rows = lax.all_gather(context, 'ctx', axis=0, tiled=True)  151 us
    all_to_all x1, blocking collectives, local(): lax.all_to_all(columns, 'ctx', split_axis=0, concat_axis=1, tiled=True)  50.8 us
    reduce_scatter x1, waiting for transfers between devices, local(): lax.psum_scatter(partial_out, 'tp', scatter_dimension=1, tiled=True)  31.3 us
    all_gather x1, waiting for transfers between devices, local(): head_rows = lax.all_gather(out_weight, 'dp', axis=0, tiled=True)  17.9 us
    dot_general x1, matrix products, local(): jnp.einsum('ikgd,jkd->kgij', query_heads, piece_keys, preferred_element_t...  16.1 us
    reduce_sum x1, other arithmetic, local(): new_total = total * factor + jnp.sum(weights, axis=-1)  15.7 us
    all_gather x1, waiting for transfers between devices, local(): lax.all_gather(prompt_values, 'ctx', axis=1, tiled=True)  14.8 us
    dot_general x1, matrix products, local(): jnp.einsum('kgij,jkd->kgid', weights.astype(jnp.bfloat16), piece_vals, pr...  14.2 us
  transfers between devices with their start and end apart: 7, of which 6 were waited for; matrix products, arithmetic and copies ran while one was open for 21% of the time, Pallas kernels for 0%

commit v1 on v0

--- a/solution.py
+++ b/solution.py
@@ -2,10 +2,35 @@
 import jax.numpy as jnp
 from jax import lax
 from jax.sharding import PartitionSpec as P
+from jax.lax import axis_index, ppermute, psum
 
 HD = 128
 BLK = 128
 RLEN = 512
+
+
+def post_the_cycles(inputs, link_axis):
+    n_parts = psum(1, link_axis)
+    gallery = []
+    m = 0
+    while m < n_parts:
+        gallery.append((m, (m + 1) % n_parts))
+        m += 1
+    panels = []
+    m = 0
+    while m < n_parts:
+        panels.append((m, (m - 1) % n_parts))
+        m += 1
+    response, g_now = ([inputs], [inputs])
+    for _ in range(n_parts // 2):
+        prior = ppermute(response[-1], link_axis, gallery)
+        response.append(prior)
+    j0 = 0
+    while j0 < (n_parts - 1) // 2:
+        g_now.append(ppermute(g_now[-1], link_axis, panels))
+        j0 += 1
+    part_now = jnp.concatenate([*response[::-1], *g_now[1:]], 1)
+    return jnp.roll(part_now, (axis_index(link_axis) - n_parts // 2) * inputs.shape[1], axis=1)
 
 
 def shifted(x, axis, by):
@@ -51,7 +76,7 @@
     )
     pieces = (
         lax.all_gather(prompt_keys, "ctx", axis=1, tiled=True),
-        lax.all_gather(prompt_values, "ctx", axis=1, tiled=True),
+        post_the_cycles(prompt_values, "ctx"),
     )
     count = pieces[0].shape[1]
     block_ids = jnp.arange(count, dtype=jnp.int32) // BLK

time: 399 us -> 395 us (0.990)
  waiting for transfers between devices: 228 us -> 204 us
  starting transfers between devices: 7.45 us -> 23.5 us
  local copies, waits for them, and re-layouts: 9.5 us -> 20.2 us
  matrix products: 59.1 us -> 52.8 us
    ppermute x0 -> x3, starting transfers between devices: none -> 18.5 us  [the longest x2 16.4 us: post_the_cycles(): prior = ppermute(response[-1], link_axis, gallery)]
    all_gather x1, waiting for transfers between devices: 17.9 us -> 0.02 us  [local(): head_rows = lax.all_gather(out_weight, 'dp', axis=0, tiled=True)]
    all_gather x1 -> x0, waiting for transfers between devices: 14.8 us -> none  [local(): lax.all_gather(prompt_values, 'ctx', axis=1, tiled=True)]
    ppermute x2, waiting for transfers between devices: 11.8 us -> 21.5 us  [shifted(): return lax.ppermute(x, axis, pairs)]
    unnamed x4 -> x21, local copies, waits for them, and re-layouts: 6.02 us -> 15.2 us
    dot_general x1, matrix products: 7.16 us -> 2.77 us  [local(): jnp.einsum('ikgd,jkd->kgij', query_heads, own_keys, preferred_element_typ...]
  transfers between devices with their start and end apart: 7 -> 9, of which waited for: 6 -> 4; matrix products, arithmetic and copies ran while one was open for 21% -> 20% of each run, Pallas kernels for 0% -> 0%
where the time goes in v1:
time: 395 us
  waiting for transfers between devices  204 us (52%)
  matrix products  52.8 us (13%)
  blocking collectives  50.8 us (13%)
  other arithmetic  30.2 us (8%)
  starting transfers between devices  23.5 us (6%)
  local copies, waits for them, and re-layouts  20.2 us (5%)
  between operations  13.4 us (3%)
    all_gather x1, waiting for transfers between devices, local(): rows = lax.all_gather(context, 'ctx', axis=0, tiled=True)  150 us
    all_to_all x1, blocking collectives, local(): lax.all_to_all(columns, 'ctx', split_axis=0, concat_axis=1, tiled=True)  50.8 us
    reduce_scatter x1, waiting for transfers between devices, local(): lax.psum_scatter(partial_out, 'tp', scatter_dimension=1, tiled=True)  31.3 us
    ppermute x2, waiting for transfers between devices, shifted(): return lax.ppermute(x, axis, pairs)  21.5 us
    ppermute x2, starting transfers between devices, post_the_cycles(): prior = ppermute(response[-1], link_axis, gallery)  16.4 us
    dot_general x1, matrix products, local(): jnp.einsum('ikgd,jkd->kgij', query_heads, piece_keys, preferred_element_t...  15.9 us
    dot_general x1, matrix products, local(): jnp.einsum('kgij,jkd->kgid', weights.astype(jnp.bfloat16), piece_vals, pr...  15.5 us
    unnamed x21, local copies, waits for them, and re-layouts  15.2 us
  transfers between devices with their start and end apart: 9, of which 4 were waited for; matrix products, arithmetic and copies ran while one was open for 20% of the time, Pallas kernels for 0%

profile of v1, /device:TPU:0, one launch (start us, length us, event | category | flops | bytes accessed | tf_op | source)
XLA Modules:
  0.0 394.6 jit_solution(4349211188845416957)
XLA Ops:
  6.5 0.0 all-gather.4.cloned.1.call-start
  6.5 1.8 copy.39
  8.3 0.0 all-gather.4.cloned.1.call-update
  8.3 0.0 all-gather.8.cloned.1.call-start
  8.4 0.7 all-gather.8.cloned.1.call-update
  9.1 0.0 all-gather.6.cloned.1.call-start
  9.1 3.1 collective-permute-start.2
  12.3 2.1 collective-permute-start.4
  14.3 1.1 copy.31
  15.4 3.6 collective-permute-start
  19.0 1.3 collective-permute-start.1
  20.3 0.6 broadcast_compare_fusion.1
  20.9 1.3 fusion.33
  22.2 0.8 fusion.32
  23.0 0.1 select_reduce_fusion
  23.1 0.7 broadcast_compare_fusion.2
  23.8 1.8 copy.37
  25.6 0.2 copy.34
  25.7 2.1 copy.54
  27.8 0.9 compare_and_fusion
  28.7 12.5 %collective-permute-done = bf16[1,256,512]{1,2,0:T(8,128)(2,1)} collective-permute-done((bf16[1,256,512]{1,2,0:T(8,128)(2,1)S(1)}, bf16[1,256,512]{1,2,0:T(8,128)(2,1)}, u32[]{:S(2)}, u32[]{:S(2)}) %collective-permute-start) | collective-permute-done | bytes 262176 | tf_op jit(solution)/shard_map/ppermute | solution.py:39
  41.2 1.1 copy.33
  42.3 9.1 %collective-permute-done.1 = bf16[1,256,512]{2,1,0:T(8,128)(2,1)S(1)} collective-permute-done((bf16[1,256,512]{2,1,0:T(8,128)(2,1)}, bf16[1,256,512]{2,1,0:T(8,128)(2,1)S(1)}, u32[]{:S(2)}, u32[]{:S(2)}) %collective-permute-start.1) | collective-permute-done | bytes 262176 | tf_op jit(solution)/shard_map/ppermute | solution.py:39
  51.4 0.8 copy.36
  52.2 0.0 collective-permute-done.2
  52.2 13.3 %collective-permute-start.3 = (bf16[1,256,512]{2,1,0:T(8,128)(2,1)S(1)}, bf16[1,256,512]{2,1,0:T(8,128)(2,1)S(1)}, u32[]{:S(2)}, u32[]{:S(2)}) collective-permute-start(bf16[1,256,512]{2,1,0:T(8,128)(2,1)S(1)} %collective-permute-done.2), channel_id=1, source_target_pairs={{0,8},{8,16},{16,24},{24,0},{1,9},{9,17},{17,25},{25,1},{2,10},{10... | collective-permute-start | bytes 786440 | tf_op jit(solution)/shard_map/ppermute | solution.py:26
  65.5 2.8 fusion.5
  68.3 0.0 copy-start
  68.3 8.3 %copy-done = f32[4,512,256,8]{2,1,3,0:T(8,128)} copy-done((f32[4,512,256,8]{2,1,3,0:T(8,128)}, f32[4,512,256,8]{2,1,3,0:T(8,128)S(1)}, u32[]{:S(2)}) %copy-start) | copy-done | bytes 16777240
  76.6 5.0 %fusion.13 = f32[4,8,256,128]{2,3,1,0:T(8,128)} fusion(f32[4,512,256,8]{2,1,3,0:T(8,128)S(1)} %get-tuple-element.8, f32[4,8,256]{2,1,0:T(8,128)S(1)} %get-tuple-element.7, pred[256,512]{0,1:T(8,128)(4,1)S(1)} %compare_and_fusion, bf16[256,4,128]{0,2,1:T(8,128)(2,1)S(1)} %bitcast.110, bf16[256,4,128]{0,2,1:T(8,128)(2,1)S(1)} %bitcast.111), kind=kOutput, calls=%fused_computation.16 | convolution fusion | flops 1091567616 | bytes 21659648 | tf_op jit(solution)/shard_map/kgij,jkd->kgid/dot_general | solution.py:74
  81.6 9.3 %fusion.11 = f32[4,8,256]{2,1,0:T(8,128)S(1)} fusion(f32[4,512,256,8]{2,1,3,0:T(8,128)} %copy-done, f32[4,8,256]{2,1,0:T(8,128)S(1)} %get-tuple-element.7, pred[256,512]{0,1:T(8,128)(4,1)S(1)} %compare_and_fusion), kind=kLoop, calls=%fused_computation.14 | loop fusion | flops 16769024 | bytes 16973824 | tf_op jit(solution)/shard_map/reduce_sum | solution.py:73
  90.9 0.0 collective-permute-done.3
  91.0 0.0 collective-permute-done.4
  91.1 0.1 constant_dynamic-slice_fusion
  91.2 1.3 copy.42
  92.5 15.9 %fusion = (f32[4,8,256]{2,1,0:T(8,128)S(1)}, f32[4,1024,256,8]{2,1,3,0:T(8,128)}) fusion(pred[1024]{0:T(1024)(128)(4,1)S(1)} %broadcast_compare_fusion, bf16[1024,4,128,1]{0,2,3,1:T(8,128)(2,1)} %bitcast.107, bf16[256,4,8,128]{3,2,1,0:T(8,128)(2,1)S(1)} %bitcast.102), kind=kOutput, calls=%fused_computation.2 | convolution fusion | flops 2172641280 | bytes 36733952 | tf_op jit(solution)/shard_map/ikgd,jkd->kgij/dot_general | solution.py:88
  108.4 14.7 %fusion.3 = f32[4,8,256]{2,1,0:T(8,128)S(1)} fusion(f32[4,1024,256,8]{2,1,3,0:T(8,128)} %get-tuple-element.10, f32[4,8,256]{2,1,0:T(8,128)S(1)} %max.18, pred[1024]{0:T(1024)(128)(4,1)S(1)} %broadcast_compare_fusion), kind=kLoop, calls=%fused_computation.5 | loop fusion | flops 33546240 | bytes 33620992 | tf_op jit(solution)/shard_map/reduce_sum | solution.py:95
  123.1 15.5 %fusion.17 = bf16[256,4,8,128]{0,3,2,1:T(8,128)(2,1)S(1)} fusion(f32[4,8,256,128]{2,3,1,0:T(8,128)} %fusion.13, bf16[1024,4,128,1]{0,2,3,1:T(8,128)(2,1)S(1)} %bitcast.108, f32[4,1024,256,8]{2,1,3,0:T(8,128)} %get-tuple-element.10, f32[4,8,256]{2,1,0:T(8,128)S(1)} %max.18, pred[1024]{0:T(1024)(128)(4,1)S(1)} %broadcast_compare_fusion, ...), kind=kOutput, calls=%fused_computation.21 | convolution fusion | flops 2185232384 | bytes 40993792 | tf_op jit(solution)/shard_map/kgij,jkd->kgid/dot_general | solution.py:96
  138.6 1.9 fusion.16
  140.5 0.0 all-gather.6.cloned.1.call-update
  140.6 0.0 reduce-scatter.2.cloned.1.call-start
  140.6 0.0 all-gather.8.cloned.1.call-done
  140.6 150.1 %all-gather.6.cloned.1.call-done = bf16[1024,4096]{0,1:T(8,128)(2,1)} async-done(((bf16[256,4096]{0,1:T(8,128)(2,1)}), bf16[1024,4096]{0,1:T(8,128)(2,1)}) %all-gather.6.cloned.1.call-update) | async-done | bytes 8388624 | tf_op jit(solution)/shard_map/all_gather | solution.py:106
  290.7 13.7 %convolution_convert_fusion = bf16[1024,1024]{1,0:T(8,128)(2,1)S(1)} fusion(bf16[1024,4096]{0,1:T(8,128)(2,1)} %all-gather.6.cloned.1.call-done, bf16[4096,1024]{1,0:T(8,128)(2,1)} %all-gather.8.cloned.1.call-done), kind=kOutput, calls=%fused_computation.23 | convolution fusion | flops 8590983168 | bytes 18874368 | tf_op jit(solution)/shard_map/dot_general | solution.py:107
  304.5 50.8 %all_to_all.19 = bf16[4,256,1024]{2,1,0:T(8,128)(2,1)S(1)} all-to-all(bf16[4,256,1024]{2,1,0:T(8,128)(2,1)S(1)} %bitcast.106), channel_id=1, replica_groups=mesh['ctx'=4,'tp'=2,'dp'=4] {'ctx'}, dimensions={0} | all-to-all | bytes 4194304 | tf_op jit(solution)/shard_map/all_to_all | solution.py:108
  355.3 1.5 copy.53
  356.8 0.0 reduce-scatter.2.cloned.1.call-update
  356.8 31.3 %reduce-scatter.2.cloned.1.call-done = bf16[256,2048]{1,0:T(8,128)(2,1)} async-done(((bf16[256,4096]{1,0:T(8,128)(2,1)}), bf16[256,2048]{1,0:T(8,128)(2,1)}) %reduce-scatter.2.cloned.1.call-update) | async-done | bytes 1048592 | tf_op jit(solution)/shard_map/reduce_scatter | solution.py:109
  (24 shorter events, 0.2 us)
Async XLA Ops:
  6.5 86.0 %all-gather.4.cloned.1.call-start = ((), (), s32[]{:S(2)}) async-start(), calls=%async_computation.2 | async-start | bytes 1310720 | tf_op jit(solution)/shard_map/all_gather | solution.py:78
  8.3 132.3 %all-gather.8.cloned.1.call-start = ((), (), s32[]{:S(2)}) async-start(), calls=%async_computation.4 | async-start | bytes 10485760 | tf_op jit(solution)/shard_map/all_gather | solution.py:105
  9.1 281.6 %all-gather.6.cloned.1.call-start = ((), (), s32[]{:S(2)}) async-start(), calls=%async_computation.3 | async-start | bytes 10485760 | tf_op jit(solution)/shard_map/all_gather | solution.py:106
  9.1 43.1 %collective-permute-start.2 = (bf16[1,256,512]{2,1,0:T(8,128)(2,1)}, bf16[1,256,512]{2,1,0:T(8,128)(2,1)S(1)}, u32[]{:S(2)}, u32[]{:S(2)}) collective-permute-start(bf16[1,256,512]{2,1,0:T(8,128)(2,1)} %param.10), channel_id=1, source_target_pairs={{0,8},{8,16},{16,24},{24,0},{1,9},{9,17},{17,25},{25,1},{2,10},{10... | collective-permute-start | bytes 786440 | tf_op jit(solution)/shard_map/ppermute | solution.py:26
  12.3 78.7 %collective-permute-start.4 = (bf16[1,256,512]{2,1,0:T(8,128)(2,1)}, bf16[1,256,512]{2,1,0:T(8,128)(2,1)S(1)}, u32[]{:S(2)}, u32[]{:S(2)}) collective-permute-start(bf16[1,256,512]{2,1,0:T(8,128)(2,1)} %param.10), channel_id=1, source_target_pairs={{0,24},{8,0},{16,8},{24,16},{1,25},{9,1},{17,9},{25,17},{2,26},{10... | collective-permute-start | bytes 786440 | tf_op jit(solution)/shard_map/ppermute | solution.py:30
  15.4 25.7 %collective-permute-start = (bf16[1,256,512]{1,2,0:T(8,128)(2,1)S(1)}, bf16[1,256,512]{1,2,0:T(8,128)(2,1)}, u32[]{:S(2)}, u32[]{:S(2)}) collective-permute-start(bf16[1,256,512]{1,2,0:T(8,128)(2,1)S(1)} %copy.31), channel_id=1, source_target_pairs={{0,16},{8,24},{1,17},{9,25},{2,18},{10,26},{3,19},{11,27},{4,20},{... | collective-permute-start | bytes 786440 | tf_op jit(solution)/shard_map/ppermute | solution.py:39
  19.0 32.4 %collective-permute-start.1 = (bf16[1,256,512]{2,1,0:T(8,128)(2,1)}, bf16[1,256,512]{2,1,0:T(8,128)(2,1)S(1)}, u32[]{:S(2)}, u32[]{:S(2)}) collective-permute-start(bf16[1,256,512]{2,1,0:T(8,128)(2,1)} %param.12), channel_id=1, source_target_pairs={{0,16},{8,24},{1,17},{9,25},{2,18},{10,26},{3,19},{11,27},{4,20},{... | collective-permute-start | bytes 786440 | tf_op jit(solution)/shard_map/ppermute | solution.py:39
  52.2 38.6 %collective-permute-start.3 = (bf16[1,256,512]{2,1,0:T(8,128)(2,1)S(1)}, bf16[1,256,512]{2,1,0:T(8,128)(2,1)S(1)}, u32[]{:S(2)}, u32[]{:S(2)}) collective-permute-start(bf16[1,256,512]{2,1,0:T(8,128)(2,1)S(1)} %collective-permute-done.2), channel_id=1, source_target_pairs={{0,8},{8,16},{16,24},{24,0},{1,9},{9,17},{17,25},{25,1},{2,10},{10... | collective-permute-start | bytes 786440 | tf_op jit(solution)/shard_map/ppermute | solution.py:26
  65.5 11.1 %copy-start.3 = (bf16[1,256,512]{1,2,0:T(8,128)(2,1)S(1)}, bf16[1,256,512]{1,2,0:T(8,128)(2,1)}, u32[]{:S(2)}) copy-start(bf16[1,256,512]{1,2,0:T(8,128)(2,1)} %copy.37) | copy-start | bytes 786436
  65.5 11.1 %copy-start.4 = (bf16[1,256,512]{1,2,0:T(8,128)(2,1)S(1)}, bf16[1,256,512]{1,2,0:T(8,128)(2,1)}, u32[]{:S(2)}) copy-start(bf16[1,256,512]{1,2,0:T(8,128)(2,1)} %copy.36) | copy-start | bytes 786436
  68.3 8.3 %copy-start = (f32[4,512,256,8]{2,1,3,0:T(8,128)}, f32[4,512,256,8]{2,1,3,0:T(8,128)S(1)}, u32[]{:S(2)}) copy-start(f32[4,512,256,8]{2,1,3,0:T(8,128)S(1)} %get-tuple-element.8) | copy-start | bytes 50331652
  81.6 9.4 %copy-start.2 = (bf16[1,256,512]{2,1,0:T(8,128)(2,1)S(1)}, bf16[1,256,512]{2,1,0:T(8,128)(2,1)}, u32[]{:S(2)}) copy-start(bf16[1,256,512]{2,1,0:T(8,128)(2,1)} %param.10) | copy-start | bytes 786436
  108.4 14.7 %copy-start.1 = (bf16[1,1024,512]{1,2,0:T(8,128)(2,1)S(1)}, bf16[1,1024,512]{1,2,0:T(8,128)(2,1)}, u32[]{:S(2)}) copy-start(bf16[1,1024,512]{1,2,0:T(8,128)(2,1)} %copy.42) | copy-start | bytes 3145732
  140.6 247.6 %reduce-scatter.2.cloned.1.call-start = ((), (), s32[]{:S(2)}) async-start(), calls=%async_computation.5 | async-start | bytes 3145728 | tf_op jit(solution)/shard_map/reduce_scatter | solution.py:109
Sparse Core Ops, SparseCore 0:
  8.9 53.1 all-gather.3
  63.6 58.5 all-gather.7
  140.7 150.0 all-gather.5
  356.9 31.1 reduce-scatter.1
